TPU v7x, 512 devices: a whole 4x8x8 slice. The times are simulated.
512 devices in a mesh: seq: 32 (over y, z_lo, core), row: 4 (over x), col: 4 (over z_hi).
Axes of the slice: x: 4, y: 8, z: 8 (z_hi: 4, z_lo: 2; z = z_hi * 2 + z_lo), core: 2. Of those that a mesh axis runs over, the one named last changes fastest.
Arguments:
- hidden_in: bfloat16 [4, 16384, 1024], P('row', 'seq')
- qkv_weight: bfloat16 [1024, 16, 192], P(None, 'col'), may hold values from -0.1875 to 0.1875
- qkv_global_weight: bfloat16 [1024, 16, 192], P('row', 'col'), may hold values from -0.1875 to 0.1875
- out_weight: bfloat16 [1024, 1024], P('col'), may hold values from -0.75 to 0.75
- ln_gain: float32 [1024], replicated, may hold values from 0.1 to 1.9
- ln_bias: float32 [1024], replicated, may hold values from -3 to 3
- ffn_in: bfloat16 [1024, 4096], P('row', 'col'), may hold values from -0.1875 to 0.1875
- ffn_out: bfloat16 [4096, 1024], P('col', 'row'), may hold values from -0.09375 to 0.09375
- ln2_gain: float32 [1024], replicated, may hold values from 0.1 to 1.9
- ln2_bias: float32 [1024], replicated, may hold values from -3 to 3
- segment_ids: int32 [4, 16384], P('row'), may hold values from 0 to 63, never falling along the last dimension, each value on 1 to 9216 neighbouring positions
- global_pos: int32 [4, 128], P('row'), may hold values from 0 to 16383, as said below
- page_owner: int32 [4, 1024, 1], P('row', 'seq'), may hold values from 0 to 31; in each aligned block of 32 rows (0 to 31, 32 to 63, ..., all dimensions but the last counted through in order) at most 2 rows name the same one
Outputs:
- hidden_out: bfloat16 [4, 16384, 1024], P('row', ('seq', 'col'))
- page_pool: bfloat16 [4, 32, 32, 2, 16, 16, 128], P('row', 'seq', None, None, None, 'col')
Inputs may be any that keep to these rules, and one draw needn't show every extreme that they name: `segment_ids`: in each stream, prompt numbers never fall along positions and every prompt has 1 to 9216 tokens, one exactly 9216. `global_pos`: in each stream, exactly 4 distinct global positions lie in each block of 512 consecutive tokens, listed in increasing order. `page_owner`: among the 32 pages of one shard of a stream, at most 2 have the same owner.
All inputs are finite; a program needn't handle non-finite values.
Results may differ from a plain program's by a relative error of at most 0.014.
The roundings to bfloat16 on the way count: a program that leaves them out, or rounds other values in their place, can miss the bound.
Values may be sent and summed in bfloat16 or wider, within the bound.
A program may use at most 64 MiB of HBM per device.

v0:
```python
import math
import jax
import jax.numpy as jnp
from jax import lax
from jax.sharding import PartitionSpec as P

HALF = 256


def padded(block, sides, width):
    for axis, dim in sides:
        count = lax.axis_size(axis)
        forward = [(i, i + 1) for i in range(count - 1)]
        backward = [(target, source) for source, target in forward]
        low = lax.ppermute(
            lax.slice_in_dim(block, block.shape[dim] - width, None, axis=dim), axis, forward
        )
        high = lax.ppermute(lax.slice_in_dim(block, 0, width, axis=dim), axis, backward)
        block = jnp.concatenate([low, block, high], axis=dim)
    return block


def combined_all(array, axis, combine):
    everything = jax.tree.map(lambda part: lax.all_gather(part, axis), array)
    initial = jax.tree.map(lambda part: part[0], everything)

    def lap(k, so_far):
        return combine(so_far, jax.tree.map(lambda part: part[k], everything))

    return lax.fori_loop(1, lax.axis_size(axis), lap, initial)


def combine_parts(first, second):
    top = jnp.maximum(first[0], second[0])
    left = jnp.exp(first[0] - top)
    right = jnp.exp(second[0] - top)
    return (
        top,
        first[1] * left + second[1] * right,
        first[2] * left[:, :, None] + second[2] * right[:, :, None],
    )


def layer_norm(values, gain, bias):
    center = values - jnp.mean(values, axis=1, keepdims=True)
    spread = jnp.mean(center * center, axis=1, keepdims=True)
    return center * lax.rsqrt(spread + 1e-05) * gain + bias


def per_device(
    hidden_in,
    qkv_weight,
    qkv_global_weight,
    out_weight,
    ln_gain,
    ln_bias,
    ffn_in,
    ffn_out,
    ln2_gain,
    ln2_bias,
    segment_ids,
    global_pos,
    page_owner,
):
    neg = -1e30
    tokens = hidden_in[0]
    shard_len, width = tokens.shape
    heads_here = qkv_weight.shape[1]
    triple = qkv_weight.shape[2]
    head_dim = triple // 3
    n_seq = lax.axis_size("seq")
    n_col = lax.axis_size("col")
    seq_index = lax.axis_index("seq")
    col_index = lax.axis_index("col")
    base = seq_index * shard_len
    scale = 1.0 / math.sqrt(head_dim)
    qkv = jnp.dot(
        tokens, qkv_weight.reshape(width, heads_here * triple), preferred_element_type=jnp.float32
    ).astype(jnp.bfloat16)
    qkv_heads = qkv.reshape(shard_len, heads_here, triple)
    queries = qkv_heads[:, :, :head_dim]
    kv_local = qkv_heads[:, :, head_dim:]
    piece = lax.all_gather(qkv_global_weight, "row", axis=0, tiled=True)
    cols = tokens
    global_proj = jnp.dot(
        cols, piece.reshape(piece.shape[0], heads_here * triple), preferred_element_type=jnp.float32
    )
    global_heads = global_proj.astype(jnp.bfloat16).reshape(shard_len, heads_here, triple)
    global_query_local = global_heads[:, :, :head_dim]
    global_kv_local = global_heads[:, :, head_dim:]
    owners = page_owner[0, :, 0]
    n_pages = owners.shape[0]
    page_len = shard_len // n_pages
    capacity = max(2, n_pages // n_seq)
    page_order = jnp.arange(n_pages, dtype=jnp.int32)
    slot = jnp.sum(
        ((owners[:, None] == owners[None, :]) & (page_order[None, :] < page_order[:, None])).astype(
            jnp.int32
        ),
        axis=1,
    )
    target = owners * capacity + slot
    placing = (target[None, :] == jnp.arange(n_seq * capacity, dtype=jnp.int32)[:, None]).astype(
        jnp.bfloat16
    )
    outgoing = jnp.dot(
        placing,
        kv_local.reshape(n_pages, page_len * heads_here * 2 * head_dim),
        preferred_element_type=jnp.float32,
    ).astype(jnp.bfloat16)
    outgoing = outgoing.reshape(n_seq, capacity, page_len, heads_here, 2 * head_dim)
    arrived = lax.all_to_all(outgoing, "seq", split_axis=0, concat_axis=0, tiled=True)
    page_pool = arrived[None, None]
    kv_ext = padded(kv_local, (("seq", 0),), HALF)
    all_pos = global_pos[0]
    n_glob = all_pos.shape[0]
    per_shard = n_glob // n_seq
    own_pos = lax.dynamic_slice_in_dim(all_pos, seq_index * per_shard, per_shard, 0)
    local_order = jnp.arange(shard_len, dtype=jnp.int32)
    own_match = (own_pos - base)[:, None] == local_order[None, :]
    picker = own_match.astype(jnp.bfloat16)
    own_kv = jnp.dot(
        picker,
        kv_local.reshape(shard_len, heads_here * 2 * head_dim),
        preferred_element_type=jnp.float32,
    ).astype(jnp.bfloat16)
    own_query = jnp.dot(
        picker,
        global_query_local.reshape(shard_len, heads_here * head_dim),
        preferred_element_type=jnp.float32,
    ).astype(jnp.bfloat16)
    gathered = (
        lax.all_gather(own_kv, "seq", axis=0, tiled=True),
        lax.all_gather(own_query, "seq", axis=0, tiled=True),
    )
    glob_kv = gathered[0].reshape(n_glob, heads_here, 2 * head_dim)
    glob_q = gathered[1].reshape(n_glob, heads_here, head_dim)
    glob_k = glob_kv[:, :, :head_dim]
    glob_v = glob_kv[:, :, head_dim:]
    seg_all = segment_ids[0]
    glob_seg = jnp.take(seg_all, all_pos)
    seg_pad = jnp.pad(seg_all, (HALF, HALF), constant_values=-1)
    query_seg = lax.dynamic_slice_in_dim(seg_all, base, shard_len, 0)
    key_seg = lax.dynamic_slice_in_dim(seg_pad, base, shard_len + 2 * HALF, 0)
    key_pos = base - HALF + jnp.arange(shard_len + 2 * HALF, dtype=jnp.int32)
    key_flag = jnp.any(key_pos[:, None] == all_pos[None, :], axis=1)
    query_pos = base + local_order
    glob_mask = query_seg[:, None] == glob_seg[None, :]
    block = min(shard_len, 512)
    k_blk = kv_ext[0 : block + 2 * HALF, :, :head_dim]
    v_blk = kv_ext[0 : block + 2 * HALF, :, head_dim:]
    s_win = jnp.einsum("qhd,khd->hqk", queries, k_blk, preferred_element_type=jnp.float32) * scale
    s_glob = jnp.einsum("qhd,ghd->hqg", queries, glob_k, preferred_element_type=jnp.float32) * scale
    m_win = (
        (jnp.abs(query_pos[:, None] - key_pos[None, :]) <= HALF)
        & (query_seg[0:block, None] == key_seg[None, 0 : block + 2 * HALF])
        & jnp.logical_not(key_flag[None, 0 : block + 2 * HALF])
    )
    top = jnp.maximum(
        jnp.max(jnp.where(m_win, s_win, neg), axis=2),
        jnp.max(jnp.where(glob_mask, s_glob, neg), axis=2),
    )
    e_win = jnp.where(m_win, jnp.exp(s_win - top[:, :, None]), 0.0)
    e_glob = jnp.where(glob_mask, jnp.exp(s_glob - top[:, :, None]), 0.0)
    total = jnp.sum(e_win, axis=2) + jnp.sum(e_glob, axis=2)
    numer = jnp.einsum(
        "hqk,khd->qhd", e_win.astype(jnp.bfloat16), v_blk, preferred_element_type=jnp.float32
    )
    numer = numer + jnp.einsum(
        "hqg,ghd->qhd", e_glob.astype(jnp.bfloat16), glob_v, preferred_element_type=jnp.float32
    )
    pieces = (numer / jnp.transpose(total)[:, :, None]).astype(jnp.bfloat16)
    s_part = (
        jnp.einsum(
            "ghd,khd->hgk",
            glob_q,
            global_kv_local[:, :, :head_dim],
            preferred_element_type=jnp.float32,
        )
        * scale
    )
    part_mask = glob_seg[:, None] == query_seg[None, :]
    part_top = jnp.max(jnp.where(part_mask, s_part, neg), axis=2)
    e_part = jnp.where(part_mask, jnp.exp(s_part - part_top[:, :, None]), 0.0)
    part_total = jnp.sum(e_part, axis=2)
    part_acc = jnp.einsum(
        "hgk,khd->hgd",
        e_part,
        global_kv_local[:, :, head_dim:].astype(jnp.float32),
        precision=lax.Precision.HIGHEST,
    )
    merged = combined_all((part_top, part_total, part_acc), "seq", combine_parts)
    glob_out = (merged[2] / merged[1][:, :, None]).astype(jnp.bfloat16)
    own_out = lax.dynamic_slice_in_dim(glob_out, seq_index * per_shard, per_shard, 1)
    placed = jnp.einsum("gt,hgd->thd", picker, own_out, preferred_element_type=jnp.float32).astype(
        jnp.bfloat16
    )
    is_own = jnp.any(own_match, axis=0)
    attention = jnp.where(is_own[:, None, None], placed, pieces).reshape(
        shard_len, heads_here * head_dim
    )
    out_rows = shard_len // n_col
    proj = lax.psum_scatter(
        jnp.dot(attention, out_weight, preferred_element_type=jnp.float32).astype(jnp.bfloat16),
        "col",
        scatter_dimension=0,
        tiled=True,
    ).astype(jnp.float32)
    residual = lax.dynamic_slice_in_dim(tokens, col_index * out_rows, out_rows, 0).astype(
        jnp.float32
    )
    middle = layer_norm(residual + proj, ln_gain, ln_bias).astype(jnp.bfloat16)
    middle_all = lax.all_gather(middle, "col", axis=0, tiled=True)
    cols = middle_all
    ffn_pre = jnp.dot(
        cols, lax.all_gather(ffn_in, "row", axis=0, tiled=True), preferred_element_type=jnp.float32
    )
    ffn_hidden = jax.nn.gelu(ffn_pre, approximate=False).astype(jnp.bfloat16)
    down_full = lax.all_gather(ffn_out, "row", axis=1, tiled=True)
    ffn_part = lax.psum_scatter(
        jnp.dot(ffn_hidden, down_full, preferred_element_type=jnp.float32).astype(jnp.bfloat16),
        "col",
        scatter_dimension=0,
        tiled=True,
    ).astype(jnp.float32)
    second = middle.astype(jnp.float32) + ffn_part
    normed = layer_norm(second, ln2_gain, ln2_bias)
    return (normed.astype(jnp.bfloat16)[None], page_pool)


def solution(mesh):
    in_specs = (
        P("row", "seq", None),
        P(None, "col", None),
        P("row", "col", None),
        P("col", None),
        P(),
        P(),
        P("row", "col"),
        P("col", "row"),
        P(),
        P(),
        P("row", None),
        P("row", None),
        P("row", "seq", None),
    )
    out_specs = (P("row", ("seq", "col"), None), P("row", "seq", None, None, None, "col", None))
    return jax.shard_map(
        per_device, mesh=mesh, in_specs=in_specs, out_specs=out_specs, check_vma=False
    )
```

profile of v0, /device:TPU:8, one launch (start us, length us, event | category | flops | bytes accessed | tf_op | source)
XLA Modules:
  0.0 483.1 jit_solution(8521363212529290202)
XLA Ops:
  8.6 1.8 gather_fusion
  12.6 37.6 %all-gather.13.cloned.1.call-done = bf16[1024,4,192]{0,2,1:T(8,128)(2,1)} async-done(((bf16[256,4,192]{0,2,1:T(8,128)(2,1)}), bf16[1024,4,192]{0,2,1:T(8,128)(2,1)}) %all-gather.13.cloned.1.call-update) | async-done | bytes 1572880 | tf_op jit(solution)/shard_map/all_gather | solution.py:83
  50.2 3.6 convolution_convert_fusion.4
  55.4 32.3 %all-gather.3 = bf16[32,4,256]{2,1,0:T(4,128)(2,1)S(1)} all-gather(bf16[1,4,256]{2,1,0:T(4,128)(2,1)S(1)} %fusion.28), channel_id=1, replica_groups=mesh['seq'=32,'row'=4,'col'=4] {'seq'}, dimensions={0}, use_global_device_ids=true | all-gather | bytes 67584 | tf_op jit(solution)/shard_map/all_gather | solution.py:134
  90.9 3.1 convolution_convert_fusion.3
  96.2 2.2 collective-permute-start
  98.5 4.2 collective-permute-start.1
  103.5 32.5 %all-gather.6 = bf16[32,4,512]{2,1,0:T(4,128)(2,1)S(1)} all-gather(bf16[1,4,512]{2,1,0:T(4,128)(2,1)S(1)} %fusion.27), channel_id=1, replica_groups=mesh['seq'=32,'row'=4,'col'=4] {'seq'}, dimensions={0}, use_global_device_ids=true | all-gather | bytes 135168 | tf_op jit(solution)/shard_map/all_gather | solution.py:133
  138.7 1.7 select_reduce_fusion
  140.6 2.7 fusion.3
  143.7 2.1 fusion.65
  146.2 31.2 %all-gather.5 = f32[32,4,128]{2,1,0:T(4,128)S(1)} all-gather(f32[1,4,128]{2,1,0:T(4,128)S(1)} %bitcast.109), channel_id=3, replica_groups=mesh['seq'=32,'row'=4,'col'=4] {'seq'}, dimensions={0}, use_global_device_ids=true | all-gather | bytes 67584 | tf_op jit(solution)/shard_map/all_gather | solution.py:24
  177.3 31.9 %all-gather.4 = f32[32,4,128]{2,1,0:T(4,128)S(1)} all-gather(f32[1,4,128]{2,1,0:T(4,128)S(1)} %bitcast.108), channel_id=2, replica_groups=mesh['seq'=32,'row'=4,'col'=4] {'seq'}, dimensions={0}, use_global_device_ids=true | all-gather | bytes 67584 | tf_op jit(solution)/shard_map/all_gather | solution.py:24
  210.3 42.2 %while.19 = (s32[]{:T(128)}, f32[4,128]{1,0:T(4,128)S(1)}, f32[4,128]{1,0:T(4,128)S(1)}, f32[4,128,64]{2,1,0:T(8,128)S(1)}, f32[32,4,128]{2,1,0:T(4,128)S(1)}, /...) while((s32[]{:T(128)}, f32[4,128]{1,0:T(4,128)S(1)}, ...), condition=%wide.region_4.5_spmd, body=%wide.region_3.4_spmd.sunk | while | flops 101381 | bytes 938135 | solution.py:30
  253.0 2.6 convolution_convert_fusion.2
  256.8 38.2 %reduce-scatter.3.cloned.1.call-done = bf16[128,1024]{1,0:T(8,128)(2,1)} async-done(((bf16[512,1024]{1,0:T(8,128)(2,1)}), bf16[128,1024]{1,0:T(8,128)(2,1)}) %reduce-scatter.3.cloned.1.call-update) | async-done | bytes 262160 | tf_op jit(solution)/shard_map/reduce_scatter | solution.py:203
  297.3 1.8 add_convert_fusion.1
  300.3 31.9 %all-gather.17.cloned.1.call-done = bf16[1024,1024]{1,0:T(8,128)(2,1)} async-done(((bf16[256,1024]{1,0:T(8,128)(2,1)}), bf16[1024,1024]{1,0:T(8,128)(2,1)}) %all-gather.17.cloned.1.call-update) | async-done | bytes 2097168 | tf_op jit(solution)/shard_map/all_gather | solution.py:216
  332.2 42.1 %all-gather.19.cloned.1.call-done = bf16[1024,1024]{1,0:T(8,128)(2,1)} async-done(((bf16[1024,256]{1,0:T(8,128)(2,1)}), bf16[1024,1024]{1,0:T(8,128)(2,1)}) %all-gather.19.cloned.1.call-update) | async-done | bytes 2097168 | tf_op jit(solution)/shard_map/all_gather | solution.py:219
  374.3 40.8 %all-gather.15.cloned.1.call-done = bf16[512,1024]{1,0:T(8,128)(2,1)} async-done(((bf16[128,1024]{1,0:T(8,128)(2,1)}), bf16[512,1024]{1,0:T(8,128)(2,1)}) %all-gather.15.cloned.1.call-update) | async-done | bytes 1048592 | tf_op jit(solution)/shard_map/all_gather | solution.py:213
  415.1 9.8 %convolution_convert_fusion.1 = bf16[512,1024]{1,0:T(8,128)(2,1)} fusion(bf16[1024,1024]{1,0:T(8,128)(2,1)} %all-gather.19.cloned.1.call-done, bf16[512,1024]{1,0:T(8,128)(2,1)} %all-gather.15.cloned.1.call-done, bf16[1024,1024]{1,0:T(8,128)(2,1)} %all-gather.17.cloned.1.call-done), kind=kOutput, calls=%fused_computation.39 | convolution fusion | flops 2182086656 | bytes 6291456 | tf_op jit(solution)/shard_map/dot_general | solution.py:221
  426.9 37.3 %all_to_all.5 = bf16[32,2,16,4,128]{4,3,2,1,0:T(4,128)(2,1)S(1)} all-to-all(bf16[32,2,16,4,128]{4,3,2,1,0:T(4,128)(2,1)} %reshape.176), channel_id=1, replica_groups=mesh['seq'=32,'row'=4,'col'=4] {'seq'}, dimensions={0} | all-to-all | bytes 2097152 | tf_op jit(solution)/shard_map/all_to_all | solution.py:112
  464.1 7.0 %reduce-scatter.5.cloned.1.call-done = bf16[128,1024]{1,0:T(8,128)(2,1)} async-done(((bf16[512,1024]{1,0:T(8,128)(2,1)}), bf16[128,1024]{1,0:T(8,128)(2,1)}) %reduce-scatter.5.cloned.1.call-update) | async-done | bytes 262160 | tf_op jit(solution)/shard_map/reduce_scatter | solution.py:220
  473.5 1.8 fusion.87
  (219 shorter events, 67.4 us)
Async XLA Ops:
  7.2 83.7 %copy-start = (bf16[1024,4,192]{0,2,1:T(8,128)(2,1)S(1)}, bf16[1024,4,192]{0,2,1:T(8,128)(2,1)}, u32[]{:S(2)}) copy-start(bf16[1024,4,192]{0,2,1:T(8,128)(2,1)} %param.16) | copy-start | bytes 4718596
  7.2 43.0 %all-gather.13.cloned.1.call-start = ((), (), s32[]{:S(2)}) async-start(), calls=%async_computation.3 | async-start | bytes 1966080 | tf_op jit(solution)/shard_map/all_gather | solution.py:83
  7.9 201.3 %all-gather.21.cloned.1.call-start = ((), (), s32[]{:S(2)}) async-start(), calls=%async_computation.9 | async-start | bytes 4325376 | tf_op jit(solution)/shard_map/all_gather | solution.py:24
  88.2 1.0 copy-start.3
  90.9 204.2 %reduce-scatter.3.cloned.1.call-start = ((), (), s32[]{:S(2)}) async-start(), calls=%async_computation.4 | async-start | bytes 1310720 | tf_op jit(solution)/shard_map/reduce_scatter | solution.py:203
  94.0 8.7 %copy-start.2 = (s32[1,16384]{1,0:T(1,128)S(1)}, s32[1,16384]{1,0:T(1,128)}, u32[]{:S(2)}) copy-start(s32[1,16384]{1,0:T(1,128)} %param.25) | copy-start | bytes 196612
  94.0 8.8 %copy-start.10 = (s32[1,128]{1,0:T(1,128)S(1)}, s32[1,128]{1,0:T(1,128)}, u32[]{:S(2)}) copy-start(s32[1,128]{1,0:T(1,128)} %param.26) | copy-start | bytes 1540
  96.2 41.3 %collective-permute-start = (bf16[256,4,128]{0,2,1:T(8,128)(2,1)}, bf16[256,4,128]{0,2,1:T(8,128)(2,1)}, u32[]{:S(2)}, u32[]{:S(2)}) collective-permute-start(bf16[256,4,128]{0,2,1:T(8,128)(2,1)} %get-tuple-element.234), channel_id=1, source_target_pairs={{0,16},{16,32},{32,48},{48,64},{64,80},{80,96},{96,112},{112,128},... | collective-permute-start | bytes 786440 | tf_op jit(solution)/shard_map/ppermute | solution.py:15
  98.5 39.0 %collective-permute-start.1 = (bf16[256,4,128]{0,2,1:T(8,128)(2,1)S(1)}, bf16[256,4,128]{0,2,1:T(8,128)(2,1)}, u32[]{:S(2)}, u32[]{:S(2)}) collective-permute-start(bf16[256,4,128]{0,2,1:T(8,128)(2,1)S(1)} %get-tuple-element.235), channel_id=1, source_target_pairs={{16,0},{32,16},{48,32},{64,48},{80,64},{96,80},{112,96},{128,112},... | collective-permute-start | bytes 786440 | tf_op jit(solution)/shard_map/ppermute | solution.py:18
  143.7 2.1 copy-start.4
  253.0 42.0 %copy-start.5 = (bf16[1,512,1024]{2,1,0:T(8,128)(2,1)S(1)}, bf16[1,512,1024]{2,1,0:T(8,128)(2,1)}, u32[]{:S(2)}) copy-start(bf16[1,512,1024]{2,1,0:T(8,128)(2,1)} %param.15) | copy-start | bytes 3145732
  253.0 44.3 %copy-start.6 = (f32[1024]{0:T(1024)S(1)}, f32[1024]{0:T(1024)}, u32[]{:S(2)}) copy-start(f32[1024]{0:T(1024)} %param.20) | copy-start | bytes 12292
  253.0 44.3 %copy-start.7 = (f32[1024]{0:T(1024)S(1)}, f32[1024]{0:T(1024)}, u32[]{:S(2)}) copy-start(f32[1024]{0:T(1024)} %param.19) | copy-start | bytes 12292
  255.6 76.7 %all-gather.17.cloned.1.call-start = ((), (), s32[]{:S(2)}) async-start(), calls=%async_computation.6 | async-start | bytes 2621440 | tf_op jit(solution)/shard_map/all_gather | solution.py:216
  256.2 118.1 %all-gather.19.cloned.1.call-start = ((), (), s32[]{:S(2)}) async-start(), calls=%async_computation.7 | async-start | bytes 2621440 | tf_op jit(solution)/shard_map/all_gather | solution.py:219
  256.8 158.4 %all-gather.15.cloned.1.call-start = ((), (), s32[]{:S(2)}) async-start(), calls=%async_computation.5 | async-start | bytes 1310720 | tf_op jit(solution)/shard_map/all_gather | solution.py:213
  256.8 43.3 %copy-start.11 = (s32[1,32,1]{1,2,0:T(1,128)S(1)}, s32[1,32,1]{1,2,0:T(1,128)}, u32[]{:S(2)}) copy-start(s32[1,32,1]{1,2,0:T(1,128)} %param.27) | copy-start | bytes 388
  299.1 172.0 %reduce-scatter.5.cloned.1.call-start = ((), (), s32[]{:S(2)}) async-start(), calls=%async_computation.8 | async-start | bytes 1310720 | tf_op jit(solution)/shard_map/reduce_scatter | solution.py:220
  425.3 45.9 %copy-start.1 = (bf16[128,1024]{1,0:T(8,128)(2,1)S(1)}, bf16[128,1024]{1,0:T(8,128)(2,1)}, u32[]{:S(2)}) copy-start(bf16[128,1024]{1,0:T(8,128)(2,1)} %add_convert_fusion.1) | copy-start | bytes 786436
  426.9 46.6 %copy-start.8 = (f32[1024]{0:T(1024)S(1)}, f32[1024]{0:T(1024)}, u32[]{:S(2)}) copy-start(f32[1024]{0:T(1024)} %param.24) | copy-start | bytes 12292
  426.9 46.6 %copy-start.9 = (f32[1024]{0:T(1024)S(1)}, f32[1024]{0:T(1024)}, u32[]{:S(2)}) copy-start(f32[1024]{0:T(1024)} %param.23) | copy-start | bytes 12292
Sparse Core Ops, SparseCore 0:
  10.1 40.0 all-gather.12
  91.0 68.8 all-gather.20
  255.7 39.2 reduce-scatter.2
  297.2 35.0 all-gather.16
  334.4 39.8 all-gather.18
  377.1 38.0 all-gather.14
  425.0 46.1 reduce-scatter.4
where the time goes:
time: 484 us; the launch traced here: 483 us
  waiting for transfers between devices  199 us (41%)
  blocking collectives  165 us (34%)
  local copies, waits for them, and re-layouts  44.3 us (9%)
  matrix products  26.6 us (5%)
  other arithmetic  25.1 us (5%)
  between operations  14.5 us (3%)
  starting transfers between devices  6.95 us (1%)
    all_gather x2, blocking collectives, combined_all(): everything = jax.tree.map(lambda part: lax.all_gather(part, axis), array)  63.1 us
    all_gather x1, waiting for transfers between devices, per_device(): down_full = lax.all_gather(ffn_out, 'row', axis=1, tiled=True)  42.1 us
    all_gather x1, waiting for transfers between devices, per_device(): middle_all = lax.all_gather(middle, 'col', axis=0, tiled=True)  40.8 us
    reduce_scatter x1, waiting for transfers between devices, per_device(): lax.psum_scatter(jnp.dot(attention, out_weight, preferred_element_type=jn...  38.2 us
    all_gather x1, waiting for transfers between devices, per_device(): piece = lax.all_gather(qkv_global_weight, 'row', axis=0, tiled=True)  37.6 us
    all_to_all x1, blocking collectives, per_device(): lax.all_to_all(outgoing, 'seq', split_axis=0, concat_axis=0, tiled=True)  37.3 us
    all_gather x1, blocking collectives, per_device(): lax.all_gather(own_kv, 'seq', axis=0, tiled=True)  32.5 us
    dynamic_slice x62, local copies, waits for them, and re-layouts, lap(): return combine(so_far, jax.tree.map(lambda part: part[k], everything))  32.5 us
  transfers between devices with their start and end apart: 9, of which 6 were waited for; matrix products, arithmetic and copies ran while one was open for 6% of the time, Pallas kernels for 0%

commit v1 on v0

--- a/solution.py
+++ b/solution.py
@@ -5,6 +5,22 @@
 from jax.sharding import PartitionSpec as P
 
 HALF = 256
+
+
+def gather_around(x, axis, dim):
+    ways, here, step = (lax.axis_size(axis), lax.axis_index(axis), x.shape[dim])
+    lengths = [n * ways if d == dim else n for d, n in enumerate(x.shape)]
+    full = lax.dynamic_update_slice_in_dim(jnp.zeros(lengths, x.dtype), x, here * step, axis=dim)
+    going_up = going_down = x
+    for far in range(1, ways // 2 + 1):
+        going_up = lax.ppermute(going_up, axis, [(d, (d + 1) % ways) for d in range(ways)])
+        full = lax.dynamic_update_slice_in_dim(full, going_up, (here - far) % ways * step, axis=dim)
+        if 2 * far < ways:
+            going_down = lax.ppermute(going_down, axis, [(d, (d - 1) % ways) for d in range(ways)])
+            full = lax.dynamic_update_slice_in_dim(
+                full, going_down, (here + far) % ways * step, axis=dim
+            )
+    return full
 
 
 def padded(block, sides, width):
@@ -212,9 +228,7 @@
     middle = layer_norm(residual + proj, ln_gain, ln_bias).astype(jnp.bfloat16)
     middle_all = lax.all_gather(middle, "col", axis=0, tiled=True)
     cols = middle_all
-    ffn_pre = jnp.dot(
-        cols, lax.all_gather(ffn_in, "row", axis=0, tiled=True), preferred_element_type=jnp.float32
-    )
+    ffn_pre = jnp.dot(cols, gather_around(ffn_in, "row", 0), preferred_element_type=jnp.float32)
     ffn_hidden = jax.nn.gelu(ffn_pre, approximate=False).astype(jnp.bfloat16)
     down_full = lax.all_gather(ffn_out, "row", axis=1, tiled=True)
     ffn_part = lax.psum_scatter(

time: 484 us -> 456 us (0.942)
  the two profiles are of different devices: /device:TPU:8 before, /device:TPU:4 now
where the time goes in v1:
time: 456 us; the launch traced here: 455 us
  blocking collectives  170 us (37%)
  waiting for transfers between devices  151 us (33%)
  local copies, waits for them, and re-layouts  51.3 us (11%)
  matrix products  28.4 us (6%)
  other arithmetic  25.1 us (6%)
  between operations  14.5 us (3%)
  starting transfers between devices  12.9 us (3%)
    all_gather x2, blocking collectives, combined_all(): everything = jax.tree.map(lambda part: lax.all_gather(part, axis), array)  65.1 us
    all_gather x1, waiting for transfers between devices, per_device(): middle_all = lax.all_gather(middle, 'col', axis=0, tiled=True)  42 us
    all_to_all x1, blocking collectives, per_device(): lax.all_to_all(outgoing, 'seq', split_axis=0, concat_axis=0, tiled=True)  38 us
    all_gather x1, waiting for transfers between devices, per_device(): piece = lax.all_gather(qkv_global_weight, 'row', axis=0, tiled=True)  37.4 us
    reduce_scatter x1, waiting for transfers between devices, per_device(): lax.psum_scatter(jnp.dot(attention, out_weight, preferred_element_type=jn...  36.9 us
    all_gather x1, blocking collectives, per_device(): lax.all_gather(own_query, 'seq', axis=0, tiled=True)  34.4 us
    all_gather x1, blocking collectives, per_device(): lax.all_gather(own_kv, 'seq', axis=0, tiled=True)  32.9 us
    dynamic_slice x62, local copies, waits for them, and re-layouts, lap(): return combine(so_far, jax.tree.map(lambda part: part[k], everything))  32.5 us
  transfers between devices with their start and end apart: 11, of which 7 were waited for; matrix products, arithmetic and copies ran while one was open for 8% of the time, Pallas kernels for 0%

profile of v1, /device:TPU:4, one launch (start us, length us, event | category | flops | bytes accessed | tf_op | source)
XLA Modules:
  0.0 454.9 jit_solution(6258302822671567501)
XLA Ops:
  12.6 37.4 %all-gather.12.cloned.1.call-done = bf16[1024,4,192]{0,2,1:T(8,128)(2,1)} async-done(((bf16[256,4,192]{0,2,1:T(8,128)(2,1)}), bf16[1024,4,192]{0,2,1:T(8,128)(2,1)}) %all-gather.12.cloned.1.call-update) | async-done | bytes 1572880 | tf_op jit(solution)/shard_map/all_gather | solution.py:99
  50.0 3.6 convolution_convert_fusion.4
  55.2 34.4 %all-gather.3 = bf16[32,4,256]{2,1,0:T(4,128)(2,1)S(1)} all-gather(bf16[1,4,256]{2,1,0:T(4,128)(2,1)S(1)} %fusion.28), channel_id=1, replica_groups=mesh['seq'=32,'row'=4,'col'=4] {'seq'}, dimensions={0}, use_global_device_ids=true | all-gather | bytes 67584 | tf_op jit(solution)/shard_map/all_gather | solution.py:150
  92.8 3.1 convolution_convert_fusion.3
  98.1 2.9 collective-permute-start
  103.1 32.9 %all-gather.6 = bf16[32,4,512]{2,1,0:T(4,128)(2,1)S(1)} all-gather(bf16[1,4,512]{2,1,0:T(4,128)(2,1)S(1)} %fusion.27), channel_id=1, replica_groups=mesh['seq'=32,'row'=4,'col'=4] {'seq'}, dimensions={0}, use_global_device_ids=true | all-gather | bytes 135168 | tf_op jit(solution)/shard_map/all_gather | solution.py:149
  140.7 2.7 fusion.3
  143.8 2.9 fusion.65
  147.1 31.2 %all-gather.5 = f32[32,4,128]{2,1,0:T(4,128)S(1)} all-gather(f32[1,4,128]{2,1,0:T(4,128)S(1)} %bitcast.109), channel_id=3, replica_groups=mesh['seq'=32,'row'=4,'col'=4] {'seq'}, dimensions={0}, use_global_device_ids=true | all-gather | bytes 67584 | tf_op jit(solution)/shard_map/all_gather | solution.py:40
  178.2 33.9 %all-gather.4 = f32[32,4,128]{2,1,0:T(4,128)S(1)} all-gather(f32[1,4,128]{2,1,0:T(4,128)S(1)} %bitcast.108), channel_id=2, replica_groups=mesh['seq'=32,'row'=4,'col'=4] {'seq'}, dimensions={0}, use_global_device_ids=true | all-gather | bytes 67584 | tf_op jit(solution)/shard_map/all_gather | solution.py:40
  213.2 42.2 %while.19 = (s32[]{:T(128)}, f32[4,128]{1,0:T(4,128)S(1)}, f32[4,128]{1,0:T(4,128)S(1)}, f32[4,128,64]{2,1,0:T(8,128)S(1)}, f32[32,4,128]{2,1,0:T(4,128)S(1)}, /...) while((s32[]{:T(128)}, f32[4,128]{1,0:T(4,128)S(1)}, ...), condition=%wide.region_4.5_spmd, body=%wide.region_3.4_spmd.sunk | while | flops 101381 | bytes 938135 | solution.py:46
  257.0 2.5 convolution_convert_fusion.2
  260.1 36.9 %reduce-scatter.3.cloned.1.call-done = bf16[128,1024]{1,0:T(8,128)(2,1)} async-done(((bf16[512,1024]{1,0:T(8,128)(2,1)}), bf16[128,1024]{1,0:T(8,128)(2,1)}) %reduce-scatter.3.cloned.1.call-update) | async-done | bytes 262160 | tf_op jit(solution)/shard_map/reduce_scatter | solution.py:219
  301.2 3.2 collective-permute-start.2
  304.4 2.8 collective-permute-start.3
  309.6 9.9 %collective-permute-done.2 = bf16[256,1024]{1,0:T(8,128)(2,1)} collective-permute-done((bf16[256,1024]{1,0:T(8,128)(2,1)}, bf16[256,1024]{1,0:T(8,128)(2,1)}, u32[]{:S(2)}, u32[]{:S(2)}) %collective-permute-start.2) | collective-permute-done | bytes 524320 | tf_op jit(solution)/shard_map/ppermute | solution.py:16
  319.4 2.4 collective-permute-start.4
  322.9 1.9 constant_dynamic-update-slice_fusion.2
  326.7 14.5 %collective-permute-done.4 = bf16[256,1024]{1,0:T(8,128)(2,1)S(1)} collective-permute-done((bf16[256,1024]{1,0:T(8,128)(2,1)}, bf16[256,1024]{1,0:T(8,128)(2,1)S(1)}, u32[]{:S(2)}, u32[]{:S(2)}) %collective-permute-start.4) | collective-permute-done | bytes 524320 | tf_op jit(solution)/shard_map/ppermute | solution.py:16
  342.0 2.9 all-gather.16.cloned.1.call-done
  344.9 42.0 %all-gather.14.cloned.1.call-done = bf16[512,1024]{1,0:T(8,128)(2,1)} async-done(((bf16[128,1024]{1,0:T(8,128)(2,1)}), bf16[512,1024]{1,0:T(8,128)(2,1)}) %all-gather.14.cloned.1.call-update) | async-done | bytes 1048592 | tf_op jit(solution)/shard_map/all_gather | solution.py:229
  386.9 9.8 %convolution_convert_fusion.1 = bf16[512,1024]{1,0:T(8,128)(2,1)} fusion(bf16[1024,1024]{1,0:T(8,128)(2,1)} %all-gather.16.cloned.1.call-done, bf16[512,1024]{1,0:T(8,128)(2,1)} %all-gather.14.cloned.1.call-done, bf16[1024,1024]{1,0:T(8,128)(2,1)} %constant_dynamic-update-slice_fusion), kind=kOutput, calls=%fused_computation.39 | convolution fusion | flops 2182086656 | bytes 6291456 | tf_op jit(solution)/shard_map/dot_general | solution.py:235
  398.7 38.0 %all_to_all.5 = bf16[32,2,16,4,128]{4,3,2,1,0:T(4,128)(2,1)S(1)} all-to-all(bf16[32,2,16,4,128]{4,3,2,1,0:T(4,128)(2,1)} %reshape.176), channel_id=1, replica_groups=mesh['seq'=32,'row'=4,'col'=4] {'seq'}, dimensions={0} | all-to-all | bytes 2097152 | tf_op jit(solution)/shard_map/all_to_all | solution.py:128
  436.7 6.3 %reduce-scatter.5.cloned.1.call-done = bf16[128,1024]{1,0:T(8,128)(2,1)} async-done(((bf16[512,1024]{1,0:T(8,128)(2,1)}), bf16[128,1024]{1,0:T(8,128)(2,1)}) %reduce-scatter.5.cloned.1.call-update) | async-done | bytes 262160 | tf_op jit(solution)/shard_map/reduce_scatter | solution.py:234
  (229 shorter events, 81.1 us)
Async XLA Ops:
  7.2 85.7 %copy-start = (bf16[1024,4,192]{0,2,1:T(8,128)(2,1)S(1)}, bf16[1024,4,192]{0,2,1:T(8,128)(2,1)}, u32[]{:S(2)}) copy-start(bf16[1024,4,192]{0,2,1:T(8,128)(2,1)} %param.16) | copy-start | bytes 4718596
  7.2 42.8 %all-gather.12.cloned.1.call-start = ((), (), s32[]{:S(2)}) async-start(), calls=%async_computation.3 | async-start | bytes 1966080 | tf_op jit(solution)/shard_map/all_gather | solution.py:99
  7.9 204.3 %all-gather.18.cloned.1.call-start = ((), (), s32[]{:S(2)}) async-start(), calls=%async_computation.8 | async-start | bytes 4325376 | tf_op jit(solution)/shard_map/all_gather | solution.py:40
  90.1 1.0 copy-start.3
  92.8 204.2 %reduce-scatter.3.cloned.1.call-start = ((), (), s32[]{:S(2)}) async-start(), calls=%async_computation.4 | async-start | bytes 1310720 | tf_op jit(solution)/shard_map/reduce_scatter | solution.py:219
  96.0 6.5 %copy-start.2 = (s32[1,16384]{1,0:T(1,128)S(1)}, s32[1,16384]{1,0:T(1,128)}, u32[]{:S(2)}) copy-start(s32[1,16384]{1,0:T(1,128)} %param.25) | copy-start | bytes 196612
  96.0 6.6 %copy-start.11 = (s32[1,128]{1,0:T(1,128)S(1)}, s32[1,128]{1,0:T(1,128)}, u32[]{:S(2)}) copy-start(s32[1,128]{1,0:T(1,128)} %param.26) | copy-start | bytes 1540
  98.1 39.5 %collective-permute-start = (bf16[256,4,128]{0,2,1:T(8,128)(2,1)}, bf16[256,4,128]{0,2,1:T(8,128)(2,1)}, u32[]{:S(2)}, u32[]{:S(2)}) collective-permute-start(bf16[256,4,128]{0,2,1:T(8,128)(2,1)} %get-tuple-element.234), channel_id=1, source_target_pairs={{0,16},{16,32},{32,48},{48,64},{64,80},{80,96},{96,112},{112,128},... | collective-permute-start | bytes 786440 | tf_op jit(solution)/shard_map/ppermute | solution.py:31
  101.1 36.5 %collective-permute-start.1 = (bf16[256,4,128]{0,2,1:T(8,128)(2,1)S(1)}, bf16[256,4,128]{0,2,1:T(8,128)(2,1)}, u32[]{:S(2)}, u32[]{:S(2)}) collective-permute-start(bf16[256,4,128]{0,2,1:T(8,128)(2,1)S(1)} %get-tuple-element.235), channel_id=1, source_target_pairs={{16,0},{32,16},{48,32},{64,48},{80,64},{96,80},{112,96},{128,112},... | collective-permute-start | bytes 786440 | tf_op jit(solution)/shard_map/ppermute | solution.py:34
  143.8 2.9 copy-start.4
  255.5 41.5 %copy-start.5 = (bf16[1,512,1024]{2,1,0:T(8,128)(2,1)S(1)}, bf16[1,512,1024]{2,1,0:T(8,128)(2,1)}, u32[]{:S(2)}) copy-start(bf16[1,512,1024]{2,1,0:T(8,128)(2,1)} %param.15) | copy-start | bytes 3145732
  256.9 42.3 %copy-start.7 = (f32[1024]{0:T(1024)S(1)}, f32[1024]{0:T(1024)}, u32[]{:S(2)}) copy-start(f32[1024]{0:T(1024)} %param.20) | copy-start | bytes 12292
  256.9 42.3 %copy-start.8 = (f32[1024]{0:T(1024)S(1)}, f32[1024]{0:T(1024)}, u32[]{:S(2)}) copy-start(f32[1024]{0:T(1024)} %param.19) | copy-start | bytes 12292
  259.5 85.4 %all-gather.16.cloned.1.call-start = ((), (), s32[]{:S(2)}) async-start(), calls=%async_computation.6 | async-start | bytes 2621440 | tf_op jit(solution)/shard_map/all_gather | solution.py:233
  260.0 126.8 %all-gather.14.cloned.1.call-start = ((), (), s32[]{:S(2)}) async-start(), calls=%async_computation.5 | async-start | bytes 1310720 | tf_op jit(solution)/shard_map/all_gather | solution.py:229
  299.3 22.6 %copy-start.12 = (s32[1,32,1]{1,2,0:T(1,128)S(1)}, s32[1,32,1]{1,2,0:T(1,128)}, u32[]{:S(2)}) copy-start(s32[1,32,1]{1,2,0:T(1,128)} %param.27) | copy-start | bytes 388
  301.1 7.6 %copy-start.6 = (bf16[256,1024]{1,0:T(8,128)(2,1)S(1)}, bf16[256,1024]{1,0:T(8,128)(2,1)}, u32[]{:S(2)}) copy-start(bf16[256,1024]{1,0:T(8,128)(2,1)} %param.21) | copy-start | bytes 1572868
  301.1 141.9 %reduce-scatter.5.cloned.1.call-start = ((), (), s32[]{:S(2)}) async-start(), calls=%async_computation.7 | async-start | bytes 1310720 | tf_op jit(solution)/shard_map/reduce_scatter | solution.py:234
  301.2 18.3 %collective-permute-start.2 = (bf16[256,1024]{1,0:T(8,128)(2,1)}, bf16[256,1024]{1,0:T(8,128)(2,1)}, u32[]{:S(2)}, u32[]{:S(2)}) collective-permute-start(bf16[256,1024]{1,0:T(8,128)(2,1)} %param.21), channel_id=1, source_target_pairs={{0,4},{4,8},{8,12},{12,0},{1,5},{5,9},{9,13},{13,1},{2,6},{6,10},{... | collective-permute-start | bytes 1572872 | tf_op jit(solution)/shard_map/ppermute | solution.py:16
  304.4 20.4 %collective-permute-start.3 = (bf16[256,1024]{1,0:T(8,128)(2,1)}, bf16[256,1024]{1,0:T(8,128)(2,1)}, u32[]{:S(2)}, u32[]{:S(2)}) collective-permute-start(bf16[256,1024]{1,0:T(8,128)(2,1)} %param.21), channel_id=1, source_target_pairs={{0,12},{4,0},{8,4},{12,8},{1,13},{5,1},{9,5},{13,9},{2,14},{6,2},{... | collective-permute-start | bytes 1572872 | tf_op jit(solution)/shard_map/ppermute | solution.py:19
  319.4 21.7 %collective-permute-start.4 = (bf16[256,1024]{1,0:T(8,128)(2,1)}, bf16[256,1024]{1,0:T(8,128)(2,1)S(1)}, u32[]{:S(2)}, u32[]{:S(2)}) collective-permute-start(bf16[256,1024]{1,0:T(8,128)(2,1)} %collective-permute-done.2), channel_id=1, source_target_pairs={{0,4},{4,8},{8,12},{12,0},{1,5},{5,9},{9,13},{13,1},{2,6},{6,10},{... | collective-permute-start | bytes 1572872 | tf_op jit(solution)/shard_map/ppermute | solution.py:16
  397.1 45.9 %copy-start.1 = (bf16[128,1024]{1,0:T(8,128)(2,1)S(1)}, bf16[128,1024]{1,0:T(8,128)(2,1)}, u32[]{:S(2)}) copy-start(bf16[128,1024]{1,0:T(8,128)(2,1)} %add_convert_fusion.1) | copy-start | bytes 786436
  398.7 46.6 %copy-start.9 = (f32[1024]{0:T(1024)S(1)}, f32[1024]{0:T(1024)}, u32[]{:S(2)}) copy-start(f32[1024]{0:T(1024)} %param.24) | copy-start | bytes 12292
  398.7 46.6 %copy-start.10 = (f32[1024]{0:T(1024)S(1)}, f32[1024]{0:T(1024)}, u32[]{:S(2)}) copy-start(f32[1024]{0:T(1024)} %param.23) | copy-start | bytes 12292
Sparse Core Ops, SparseCore 0:
  10.1 39.8 all-gather.11
  92.9 67.9 all-gather.17
  259.6 37.3 reduce-scatter.2
  299.1 45.6 all-gather.15
  347.6 39.2 all-gather.13
  396.8 46.1 reduce-scatter.4
